TPU v7x, 128 devices: a whole 4x4x4 slice. The times are simulated.
128 devices in a mesh: az: 8 (over z_lo, y), col: 16 (over z_hi, x, core).
Axes of the slice: x: 4, y: 4, z: 4 (z_hi: 2, z_lo: 2; z = z_hi * 2 + z_lo), core: 2. Of those that a mesh axis runs over, the one named last changes fastest.
Arguments:
- phase_field: float32 [64, 1024, 2048], P(None, 'col', 'az'), may hold values from -1 to 1
- velocity: bfloat16 [2, 64, 1024, 2048], P(None, None, 'col', 'az'), may hold values from -4 to 4
- owned_modes: int32 [128, 4], replicated, may hold values from 0 to 511, as said below
- legendre: bfloat16 [512, 1024, 512], P(('az', 'col')), as said below
- radial_inverse: bfloat16 [512, 64, 64], replicated, as said below
Outputs:
- new_phase: float32 [64, 1024, 2048], P(None, 'col', 'az')
Inputs may be any that keep to these rules, and one draw needn't show every extreme that they name: `owned_modes`: every order from 0 to 511 appears exactly once; the second half of each row is 511 minus its first half. legendre[q, t, l] is the orthonormal associated Legendre function of degree l and order m_q (owned_modes flattened at q) at cos(theta_t), normalized so that the integral of its square times sin(theta) over theta is 1, rounded to bfloat16; it is 0 for l < m_q. `radial_inverse`: one matrix for each degree.
All inputs are finite; a program needn't handle non-finite values.
Results may differ from a plain program's by a relative error of at most 0.0003.
Values sent between devices are 32-bit elements; how exact they have to be, the bound alone decides.
No kernel may reach another device: no remote copies, remote signals or barrier semaphores. Data moves between devices by JAX's collectives and lax.ppermute only.
A program may use at most 192 MiB of HBM per device.

v0:
```python
import math
import jax
import jax.numpy as jnp
from jax import lax
from jax.sharding import PartitionSpec as P

step_time = 0.002
mobility_step = 4e-06
highest_precision = lax.Precision.HIGHEST


def padded_2(block, sides, width):
    for axis, dim in sides:
        count = lax.axis_size(axis)
        forward = [(i, i + 1) for i in range(count - 1)]
        forward.append((count - 1, 0))
        backward = [(target, source) for source, target in forward]
        low = lax.ppermute(
            lax.slice_in_dim(block, block.shape[dim] - width, None, axis=dim), axis, forward
        )
        high = lax.ppermute(lax.slice_in_dim(block, 0, width, axis=dim), axis, backward)
        block = jnp.concatenate([low, block, high], axis=dim)
    return block


def shell_radii(shells):
    return 0.75 + 0.25 * (jnp.arange(shells, dtype=jnp.float32) + 0.5) / shells


def colat_weights(count):
    row_index = jnp.arange(count, dtype=jnp.int32)
    waves = jnp.arange(1, count // 2 + 1, dtype=jnp.int32)
    turns = (2 * row_index[:, None] + 1) * waves[None, :] % (2 * count)
    cosines = jnp.cos(turns.astype(jnp.float32) * (math.pi / count))
    wave_float = waves.astype(jnp.float32)
    coefs = 1.0 / (4.0 * wave_float * wave_float - 1.0)
    return 2.0 / count * (1.0 - 2.0 * jnp.dot(cosines, coefs, precision=highest_precision))


def forward_waves(phi_index, mode_list, phi_count):
    turns = phi_index[:, None] * mode_list[None, :] % phi_count
    angle = turns.astype(jnp.float32) * (2.0 * math.pi / phi_count)
    return jnp.stack([jnp.cos(angle), -jnp.sin(angle)], axis=1) / phi_count


def inverse_waves(mode_list, phi_count):
    phi_index = jnp.arange(phi_count, dtype=jnp.int32)
    turns = mode_list[:, None] * phi_index[None, :] % phi_count
    angle = turns.astype(jnp.float32) * (2.0 * math.pi / phi_count)
    doubling = jnp.where(mode_list == 0, 1.0, 2.0).astype(jnp.float32)[:, None]
    return jnp.stack([doubling * jnp.cos(angle), -doubling * jnp.sin(angle)], axis=0)


def body(phase_field, velocity, owned_modes, legendre, radial_inverse):
    shells, theta_local, phi_local = phase_field.shape
    az_count = lax.axis_size("az")
    col_count = lax.axis_size("col")
    phi_count = phi_local * az_count
    theta_count = theta_local * col_count
    theta_block = theta_local // az_count
    mode_list = owned_modes.reshape(-1)
    mode_count = mode_list.shape[0]
    mode_dev = legendre.shape[0]
    degree_count = legendre.shape[2]
    legendre_full = legendre.astype(jnp.float32)
    shell_radius = shell_radii(shells)
    padded = padded_2(phase_field, (("az", 2), ("col", 1)), 1)
    col_here = lax.axis_index("col")
    row_index = jnp.arange(theta_local + 2, dtype=jnp.int32)
    row_mask = jnp.logical_not(
        jnp.logical_or(
            jnp.logical_and(row_index == 0, col_here == 0),
            jnp.logical_and(row_index == theta_local + 1, col_here == col_count - 1),
        )
    )
    padded = padded * row_mask.astype(jnp.float32)[None, :, None]
    centre_rows = padded[:, 1:-1, :]
    east_cell = centre_rows[:, :, 2:]
    west_cell = centre_rows[:, :, :-2]
    south_cell = padded[:, 2:, 1:-1]
    north_cell = padded[:, :-2, 1:-1]
    d_phi = (east_cell - west_cell) * (phi_count / (4.0 * math.pi))
    d_theta = (south_cell - north_cell) * (theta_count / (2.0 * math.pi))
    spin_rate = velocity[0].astype(jnp.float32)
    sweep_speed = velocity[1].astype(jnp.float32)
    advected = phase_field - step_time * (
        spin_rate * d_phi + sweep_speed / shell_radius[:, None, None] * d_theta
    )
    potential = phase_field * phase_field * phase_field - phase_field
    fields = jnp.stack([advected, potential])
    wave_table = forward_waves(jnp.arange(phi_count, dtype=jnp.int32), mode_list, phi_count)
    spectra = jnp.einsum(
        "frtp,pqk->ktqfr",
        lax.all_to_all(fields, "az", split_axis=2, concat_axis=3, tiled=True),
        wave_table,
        precision=highest_precision,
    )
    spectra = spectra.reshape(mode_count, theta_block, 4 * shells)
    gathered = lax.all_to_all(spectra, ("az", "col"), split_axis=0, concat_axis=1, tiled=True)
    gathered = gathered.reshape(mode_dev, az_count, col_count, theta_block, 4 * shells)
    gathered = jnp.transpose(gathered, (0, 2, 1, 3, 4))
    gathered = gathered.reshape(mode_dev, theta_count, 4 * shells)
    weights = colat_weights(theta_count)
    weighted = gathered * weights[None, :, None]
    coeffs = jnp.einsum("ktx,ktl->klx", weighted, legendre_full, precision=highest_precision)
    coeffs = coeffs.reshape(mode_dev, degree_count, 2, 2, shells)
    degrees = jnp.arange(degree_count, dtype=jnp.float32)
    factor = (
        mobility_step
        * (degrees * (degrees + 1.0))[:, None]
        / (shell_radius * shell_radius)[None, :]
    )
    right_side = coeffs[:, :, :, 0, :] - factor[None, :, None, :] * coeffs[:, :, :, 1, :]
    solved = jnp.einsum(
        "lrs,klqs->klqr",
        radial_inverse.astype(jnp.float32),
        right_side,
        precision=highest_precision,
    )
    synthesis = jnp.einsum(
        "ktl,klx->ktx",
        legendre_full,
        solved.reshape(mode_dev, degree_count, 2 * shells),
        precision=highest_precision,
    )
    synthesis = synthesis.reshape(mode_dev, col_count, az_count, theta_block, 2 * shells)
    synthesis = jnp.transpose(synthesis, (0, 2, 1, 3, 4)).reshape(mode_dev, theta_count, 2 * shells)
    grid_modes = lax.all_to_all(synthesis, ("az", "col"), split_axis=1, concat_axis=0, tiled=True)
    grid_modes = grid_modes.reshape(mode_count, theta_block, 2, shells)
    inverse_table = inverse_waves(mode_list, phi_count)
    row_fields = jnp.einsum("ktqr,qkp->rtp", grid_modes, inverse_table, precision=highest_precision)
    new_phase = lax.all_to_all(row_fields, "az", split_axis=2, concat_axis=1, tiled=True)
    return new_phase


def solution(mesh):
    in_specs = (
        P(None, "col", "az"),
        P(None, None, "col", "az"),
        P(),
        P(("az", "col"), None, None),
        P(),
    )
    out_specs = P(None, "col", "az")
    return jax.shard_map(body, mesh=mesh, in_specs=in_specs, out_specs=out_specs, check_vma=False)
```

profile of v0, /device:TPU:0, one launch (start us, length us, event | category | flops | bytes accessed | tf_op | source)
XLA Modules:
  0.0 518.3 jit_solution(17031054977183519346)
XLA Ops:
  0.0 4.2 fusion.74
  4.2 2.3 copy.81
  6.5 1.7 collective-permute-start
  8.2 0.7 copy.82
  8.9 2.9 collective-permute-start.1
  11.7 4.8 fusion.73
  16.5 4.4 copy.50
  21.0 0.0 collective-permute-done
  21.0 1.9 copy.46
  22.9 0.0 collective-permute-done.1
  22.9 2.9 copy.48
  25.8 1.2 pad_maximum_fusion.3
  27.0 0.1 collective-permute-start.2
  27.1 5.6 %collective-permute-start.3 = (f32[64,1,258]{2,0,1:T(8,128)S(1)}, f32[64,1,258]{2,0,1:T(8,128)S(1)}, u32[]{:S(2)}, u32[]{:S(2)}) collective-permute-start(f32[64,1,258]{2,0,1:T(8,128)S(1)} %get-tuple-element.6), channel_id=1, source_target_pairs={{1,0},{2,1},{3,2},{4,3},{5,4},{6,5},{7,6},{8,7},{9,8},{10,9},{11,1... | collective-permute-start | bytes 198152 | tf_op jit(solution)/shard_map/ppermute | solution.py:21
  32.7 2.0 collective-permute-done.2
  34.7 0.2 collective-permute-done.3
  34.9 3.1 maximum_multiply_fusion.1
  38.1 0.0 copy-done.1
  38.1 10.6 %fusion.20 = (f32[1,64,64,256]{3,1,0,2:T(8,128)S(1)}, f32[1,64,64,256]{3,1,0,2:T(8,128)}) fusion(f32[64,66,258]{2,0,1:T(8,128)S(1)} %maximum_multiply_fusion.1, bf16[1,64,64,256]{3,2,1,0:T(8,128)(2,1)} %get-tuple-element.10, bf16[1,64,64,256]{3,2,1,0:T(8,128)(2,1)} %get-tuple-element.9, f32[64]{0:T(128)S(1)} %multiply_add_fusion.1, ...), kind=kLoop, calls=%fused_computation.32 | loop fusion | flops 15728640 | bytes 33554688 | tf_op jit(solution)/shard_map/stack | solution.py:90
  48.7 6.3 %pad_maximum_fusion = f32[2,64,64,256]{3,1,0,2:T(8,128)} fusion(f32[1,64,64,256]{3,1,0,2:T(8,128)} %get-tuple-element.8, f32[1,64,64,256]{3,1,0,2:T(8,128)S(1)} %get-tuple-element.7), kind=kLoop, calls=%fused_computation.9 | loop fusion | flops 2097152 | bytes 16777216 | tf_op jit(solution)/shard_map/stack | solution.py:90
  55.0 5.6 %all-to-all-start = ((f32[2,64,64,256]{3,1,0,2:T(8,128)}), f32[2,64,64,256]{3,1,0,2:T(8,128)}, u32[]{:S(2)}, u32[]{:S(2)}) async-start(f32[2,64,64,256]{3,1,0,2:T(8,128)} %pad_maximum_fusion), calls=%async_computation | async-start | bytes 16777216 | tf_op jit(solution)/shard_map/all_to_all | solution.py:94
  60.6 0.0 copy-done.5
  60.6 0.1 copy.42
  60.7 0.1 reshape.391
  60.8 18.0 %fusion.47 = (f32[2048,1,512]{2,0,1:T(8,128)}, f32[2048,1,512]{2,0,1:T(8,128)}) fusion(s32[512]{0:T(512)S(1)} %reshape.391), kind=kLoop, calls=%fused_computation.68 | loop fusion | flops 15728640 | bytes 8390656 | tf_op jit(solution)/shard_map/cos | solution.py:43
  78.9 75.0 %all-to-all-done = f32[2,64,64,256]{3,1,0,2:T(8,128)} async-done(((f32[2,64,64,256]{3,1,0,2:T(8,128)}), f32[2,64,64,256]{3,1,0,2:T(8,128)}, u32[]{:S(2)}, u32[]{:S(2)}) %all-to-all-start) | async-done | bytes 8388640 | tf_op jit(solution)/shard_map/all_to_all | solution.py:94
  153.8 13.2 %copy.100 = f32[2,64,8,8,256]{4,2,1,3,0:T(8,128)} copy(f32[2,64,8,8,256]{4,1,0,3,2:T(8,128)} %bitcast.6) | data formatting | bytes 16777216 | tf_op jit(solution)/shard_map/all_to_all | solution.py:94
  167.0 9.3 %reshape.403 = f32[2,64,8,2048,1]{3,1,2,0,4:T(8,128)} reshape(f32[2,64,8,8,256]{4,3,1,2,0:T(8,128)} %bitcast.103) | data formatting | bytes 16777216 | tf_op jit(solution)/shard_map/all_to_all | solution.py:94
  176.3 32.7 %fusion.34 = f32[512,8,2,2,64]{0,4,1,3,2:T(8,128)S(1)} fusion(f32[2,64,8,2048,1]{3,1,2,0,4:T(8,128)} %reshape.403, f32[2048,1,512]{2,0,1:T(8,128)} %get-tuple-element.20, f32[2048,1,512]{2,0,1:T(8,128)} %get-tuple-element.19), kind=kOutput, calls=%fused_computation.55 | convolution fusion | flops 25773998080 | bytes 20971520 | tf_op jit(solution)/shard_map/frtp,pqk->ktqfr/dot_general | solution.py:92
  209.1 2.5 copy.56
  211.5 5.4 %copy.57 = f32[512,8,256]{2,1,0:T(8,128)} copy(f32[512,8,256]{0,2,1:T(8,128)} %bitcast.104) | data formatting | bytes 8388608 | tf_op jit(solution)/shard_map/reshape | solution.py:98
  217.0 40.8 %all-to-all-start.1 = ((f32[512,8,256]{2,1,0:T(8,128)}), f32[512,8,256]{2,1,0:T(8,128)}, u32[]{:S(2)}, u32[]{:S(2)}) async-start(f32[512,8,256]{2,1,0:T(8,128)} %copy.57), calls=%async_computation.1 | async-start | bytes 8388608 | tf_op jit(solution)/shard_map/all_to_all | solution.py:99
  257.8 13.0 %copy.75 = bf16[512,64,64,1]{2,1,3,0:T(8,128)(2,1)} copy(bf16[512,64,64,1]{0,2,1,3:T(8,128)(2,1)} %bitcast.109) | data formatting | bytes 8388608 | tf_op args[4]
  270.8 9.9 %fusion.40 = f32[1,1024]{1,0:T(1,128)S(1)} fusion(f32[512,1]{0,1:T(1,128)S(1)} %bitcast.112, s32[512]{0:T(512)S(1)} %iota_add_fusion, s32[1024]{0:T(1024)S(1)} %multiply_add_fusion), kind=kOutput, calls=%fused_computation.59 | convolution fusion | flops 13631488 | bytes 12288 | tf_op jit(solution)/shard_map/dot_general | solution.py:37
  280.7 0.2 broadcast_divide_fusion
  280.9 29.5 %all-to-all-done.1 = f32[512,8,256]{2,1,0:T(8,128)} async-done(((f32[512,8,256]{2,1,0:T(8,128)}), f32[512,8,256]{2,1,0:T(8,128)}, u32[]{:S(2)}, u32[]{:S(2)}) %all-to-all-start.1) | async-done | bytes 4194336 | tf_op jit(solution)/shard_map/all_to_all | solution.py:99
  310.4 2.7 copy.59
  313.1 0.0 copy-start.4
  313.1 0.6 bitcast_multiply_fusion
  313.7 1.6 copy-done.4
  315.3 3.5 fusion.76
  318.8 1.2 fusion.75
  319.9 2.1 copy.84
  322.0 1.8 copy.85
  323.8 17.1 %fusion.51 = f32[4,512,2,64]{3,0,2,1:T(4,128)} fusion(bf16[512,64,64,1]{2,1,3,0:T(8,128)(2,1)} %copy.75, f32[4,512,2,1,64]{4,0,2,1,3:T(4,128)} %copy.85, f32[4,512,2,1,64]{4,0,2,1,3:T(4,128)S(1)} %copy.84, f32[512,64]{1,0:T(8,128)S(1)} %broadcast_divide_fusion), kind=kOutput, calls=%fused_computation.73 | convolution fusion | flops 201850880 | bytes 7471104 | tf_op jit(solution)/shard_map/lrs,klqs->klqr/dot_general | solution.py:114
  340.9 1.9 copy.64
  342.8 6.4 %convolution_bitcast_fusion = f32[4,1024,128]{1,2,0:T(8,128)S(1)} fusion(f32[4,512,128]{1,2,0:T(8,128)S(1)} %bitcast.110, bf16[4,1024,512]{2,1,0:T(8,128)(2,1)} %param.8), kind=kOutput, calls=%fused_computation.72 | convolution fusion | flops 3221225472 | bytes 7340032 | tf_op jit(solution)/shard_map/ktl,klx->ktx/dot_general | solution.py:120
  349.2 1.8 copy.65
  351.0 1.8 copy.66
  352.9 2.7 copy.67
  355.5 5.8 %all-to-all-start.2 = ((f32[4,1024,128]{2,0,1:T(4,128)}), f32[4,1024,128]{2,0,1:T(4,128)S(1)}, u32[]{:S(2)}, u32[]{:S(2)}) async-start(f32[4,1024,128]{2,0,1:T(4,128)} %copy.67), calls=%async_computation.2 | async-start | bytes 4194304 | tf_op jit(solution)/shard_map/all_to_all | solution.py:128
  361.3 19.1 %cosine_multiply_fusion = (f32[1,512,2048]{2,1,0:T(8,128)}, f32[1,512,2048]{2,1,0:T(8,128)}) fusion(s32[512]{0:T(512)S(1)} %reshape.391, f32[512]{0:T(512)S(1)} %get-tuple-element.17, f32[512]{0:T(512)S(1)} %get-tuple-element.18), kind=kLoop, calls=%fused_computation.44 | loop fusion | flops 16777216 | bytes 8394752 | tf_op jit(solution)/shard_map/mul | solution.py:51
  380.4 11.3 %all-to-all-done.2 = f32[4,1024,128]{2,0,1:T(4,128)S(1)} async-done(((f32[4,1024,128]{2,0,1:T(4,128)}), f32[4,1024,128]{2,0,1:T(4,128)S(1)}, u32[]{:S(2)}, u32[]{:S(2)}) %all-to-all-start.2) | async-done | bytes 2097184 | tf_op jit(solution)/shard_map/all_to_all | solution.py:128
  391.7 0.1 copy.101
  391.9 0.3 copy.69
  392.1 3.7 reshape.399
  395.8 21.0 %fusion.31 = f32[64,8,2048]{2,0,1:T(8,128)} fusion(f32[512,8,2,64]{3,2,1,0:T(2,128)} %reshape.399, f32[1,512,2048]{2,1,0:T(8,128)} %get-tuple-element.16, f32[1,512,2048]{2,1,0:T(8,128)} %get-tuple-element.15), kind=kOutput, calls=%fused_computation.52 | convolution fusion | flops 12886999040 | bytes 14680064 | tf_op jit(solution)/shard_map/ktqr,qkp->rtp/dot_general | solution.py:131
  416.8 7.0 %copy.71 = f32[64,8,2048]{0,1,2:T(8,128)} copy(f32[64,8,2048]{2,0,1:T(8,128)} %fusion.31) | data formatting | bytes 8388608 | tf_op jit(solution)/shard_map/ktqr,qkp->rtp/transpose | solution.py:131
  423.8 10.0 %reshape.410 = f32[8,1,131072]{2,1,0:T(1,128)} reshape(f32[2048,8,64]{2,1,0:T(8,128)} %bitcast.101) | data formatting | bytes 8388608
  433.8 53.7 %all_to_all.66 = f32[8,1,131072]{2,1,0:T(1,128)} all-to-all(f32[8,1,131072]{2,1,0:T(1,128)} %reshape.410), channel_id=1, replica_groups=mesh['az'=8,'col'=16] {'az'}, dimensions={0} | all-to-all | bytes 8388608 | tf_op jit(solution)/shard_map/all_to_all | solution.py:132
  487.5 0.6 broadcast.379
  488.1 13.8 %reduce = f32[8,131072]{1,0:T(8,128)} reduce(f32[8,1,131072]{2,1,0:T(1,128)} %all_to_all.66, f32[]{:T(128)} %broadcast.379), dimensions={1}, to_apply=%all_to_all.58.reduce_sub_computation | reduce | bytes 8388612 | tf_op jit(solution)/shard_map/all_to_all | solution.py:132
  501.8 8.7 %reshape.411 = f32[2048,8,64]{2,1,0:T(8,128)} reshape(f32[8,131072]{1,0:T(8,128)} %reduce) | data formatting | bytes 8388608
  510.5 7.6 %copy.72 = f32[64,8,8,256]{3,2,1,0:T(8,128)} copy(f32[64,8,8,256]{0,2,3,1:T(8,128)} %bitcast.102) | data formatting | bytes 8388608 | tf_op jit(solution)/shard_map/all_to_all | solution.py:132
  (17 shorter events, 0.1 us)
Async XLA Ops:
  6.5 14.5 %collective-permute-start = (f32[64,64,1]{1,0,2:T(8,128)S(1)}, f32[64,64,1]{1,0,2:T(8,128)S(1)}, u32[]{:S(2)}, u32[]{:S(2)}) collective-permute-start(f32[64,64,1]{1,0,2:T(8,128)S(1)} %copy.81), channel_id=1, source_target_pairs={{0,16},{16,32},{32,48},{48,64},{64,80},{80,96},{96,112},{112,0},{1... | collective-permute-start | bytes 49160 | tf_op jit(solution)/shard_map/ppermute | solution.py:18
  8.9 7.6 %copy-start = (f32[64,64,256]{2,1,0:T(8,128)S(1)}, f32[64,64,256]{2,1,0:T(8,128)}, u32[]{:S(2)}) copy-start(f32[64,64,256]{2,1,0:T(8,128)} %param.5) | copy-start | bytes 12582916
  8.9 14.0 %collective-permute-start.1 = (f32[64,64,1]{1,0,2:T(8,128)S(1)}, f32[64,64,1]{1,0,2:T(8,128)S(1)}, u32[]{:S(2)}, u32[]{:S(2)}) collective-permute-start(f32[64,64,1]{1,0,2:T(8,128)S(1)} %copy.82), channel_id=1, source_target_pairs={{16,0},{32,16},{48,32},{64,48},{80,64},{96,80},{112,96},{0,112},{1... | collective-permute-start | bytes 49160 | tf_op jit(solution)/shard_map/ppermute | solution.py:21
  25.8 9.1 %copy-start.2 = (f32[64,64,256]{2,0,1:T(8,128)S(1)}, f32[64,64,256]{2,0,1:T(8,128)}, u32[]{:S(2)}) copy-start(f32[64,64,256]{2,0,1:T(8,128)} %copy.50) | copy-start | bytes 12582916
  25.8 9.1 %copy-start.3 = (f32[64,64,1]{2,0,1:T(8,128)S(1)}, f32[64,64,1]{2,0,1:T(8,128)}, u32[]{:S(2)}) copy-start(f32[64,64,1]{2,0,1:T(8,128)} %copy.48) | copy-start | bytes 49156
  27.0 7.7 %collective-permute-start.2 = (f32[64,1,258]{2,0,1:T(8,128)S(1)}, f32[64,1,258]{2,0,1:T(8,128)S(1)}, u32[]{:S(2)}, u32[]{:S(2)}) collective-permute-start(f32[64,1,258]{2,0,1:T(8,128)S(1)} %get-tuple-element.5), channel_id=1, source_target_pairs={{0,1},{1,2},{2,3},{3,4},{4,5},{5,6},{6,7},{7,8},{8,9},{9,10},{10,1... | collective-permute-start | bytes 198152 | tf_op jit(solution)/shard_map/ppermute | solution.py:18
  27.1 7.8 %collective-permute-start.3 = (f32[64,1,258]{2,0,1:T(8,128)S(1)}, f32[64,1,258]{2,0,1:T(8,128)S(1)}, u32[]{:S(2)}, u32[]{:S(2)}) collective-permute-start(f32[64,1,258]{2,0,1:T(8,128)S(1)} %get-tuple-element.6), channel_id=1, source_target_pairs={{1,0},{2,1},{3,2},{4,3},{5,4},{6,5},{7,6},{8,7},{9,8},{10,9},{11,1... | collective-permute-start | bytes 198152 | tf_op jit(solution)/shard_map/ppermute | solution.py:21
  32.7 5.4 %copy-start.1 = (f32[64,64,256]{2,1,0:T(8,128)S(1)}, f32[64,64,256]{2,1,0:T(8,128)}, u32[]{:S(2)}) copy-start(f32[64,64,256]{2,1,0:T(8,128)} %param.5) | copy-start | bytes 12582916
  55.0 5.6 %copy-start.5 = (s32[128,4]{0,1:T(4,128)S(1)}, s32[128,4]{0,1:T(4,128)}, u32[]{:S(2)}) copy-start(s32[128,4]{0,1:T(4,128)} %param.7) | copy-start | bytes 6148
  55.0 98.8 %all-to-all-start = ((f32[2,64,64,256]{3,1,0,2:T(8,128)}), f32[2,64,64,256]{3,1,0,2:T(8,128)}, u32[]{:S(2)}, u32[]{:S(2)}) async-start(f32[2,64,64,256]{3,1,0,2:T(8,128)} %pad_maximum_fusion), calls=%async_computation | async-start | bytes 16777216 | tf_op jit(solution)/shard_map/all_to_all | solution.py:94
  217.0 93.4 %all-to-all-start.1 = ((f32[512,8,256]{2,1,0:T(8,128)}), f32[512,8,256]{2,1,0:T(8,128)}, u32[]{:S(2)}, u32[]{:S(2)}) async-start(f32[512,8,256]{2,1,0:T(8,128)} %copy.57), calls=%async_computation.1 | async-start | bytes 8388608 | tf_op jit(solution)/shard_map/all_to_all | solution.py:99
  313.1 2.2 copy-start.4
  355.5 36.2 %all-to-all-start.2 = ((f32[4,1024,128]{2,0,1:T(4,128)}), f32[4,1024,128]{2,0,1:T(4,128)S(1)}, u32[]{:S(2)}, u32[]{:S(2)}) async-start(f32[4,1024,128]{2,0,1:T(4,128)} %copy.67), calls=%async_computation.2 | async-start | bytes 4194304 | tf_op jit(solution)/shard_map/all_to_all | solution.py:128
where the time goes:
time: 526 us; the launch traced here: 518 us
  local copies, waits for them, and re-layouts  120 us (23%)
  waiting for transfers between devices  118 us (22%)
  matrix products  90.6 us (17%)
  other arithmetic  73 us (14%)
  starting transfers between devices  62.4 us (12%)
  blocking collectives  53.7 us (10%)
    all_to_all x1, waiting for transfers between devices, body(): lax.all_to_all(fields, 'az', split_axis=2, concat_axis=3, tiled=True)  75 us
    all_to_all x1, blocking collectives, body(): lax.all_to_all(row_fields, 'az', split_axis=2, concat_axis=1, tiled=True)  53.7 us
    unnamed x21, local copies, waits for them, and re-layouts  44.6 us
    all_to_all x1, starting transfers between devices, body(): lax.all_to_all(spectra, ('az', 'col'), split_axis=0, concat_axis=1, tiled...  40.8 us
    dot_general x1, matrix products, body(): jnp.einsum('frtp,pqk->ktqfr', lax.all_to_all(fields, 'az', split_axis=2,...  32.7 us
    all_to_all x1, waiting for transfers between devices, body(): lax.all_to_all(spectra, ('az', 'col'), split_axis=0, concat_axis=1, tiled...  29.5 us
    all_to_all x2, local copies, waits for them, and re-layouts, body(): lax.all_to_all(fields, 'az', split_axis=2, concat_axis=3, tiled=True)  22.5 us
    dot_general x1, matrix products, body(): jnp.einsum('ktqr,qkp->rtp', grid_modes, inverse_table, precision=highest_...  21 us
  transfers between devices with their start and end apart: 7, of which 5 were waited for; matrix products, arithmetic and copies ran while one was open for 14% of the time, Pallas kernels for 0%

commit v1 on v0

--- a/solution.py
+++ b/solution.py
@@ -129,7 +129,10 @@
     grid_modes = grid_modes.reshape(mode_count, theta_block, 2, shells)
     inverse_table = inverse_waves(mode_list, phi_count)
     row_fields = jnp.einsum("ktqr,qkp->rtp", grid_modes, inverse_table, precision=highest_precision)
-    new_phase = lax.all_to_all(row_fields, "az", split_axis=2, concat_axis=1, tiled=True)
+    new_phase = jnp.concatenate(
+        lax.all_to_all(jnp.stack(jnp.split(row_fields, lax.axis_size("az"), axis=2)), "az", 0, 0),
+        axis=1,
+    )
     return new_phase
 
 

time: 526 us -> 480 us (0.913)
  local copies, waits for them, and re-layouts: 120 us -> 91.2 us
  other arithmetic: 73 us -> 59.2 us
    unnamed x21 -> x26, local copies, waits for them, and re-layouts: 44.6 us -> 26.2 us
    all_to_all x1 -> x0, other arithmetic: 13.8 us -> none  [body(): lax.all_to_all(row_fields, 'az', split_axis=2, concat_axis=1, tiled=True)]
    all_to_all x2 -> x0, local copies, waits for them, and re-layouts: 8.14 us -> none  [body(): lax.all_to_all(row_fields, 'az', split_axis=2, concat_axis=1, tiled=True)]
    transpose x1 -> x0, local copies, waits for them, and re-layouts: 6.98 us -> none  [body(): jnp.einsum('ktqr,qkp->rtp', grid_modes, inverse_table, precision=highest_...]
  transfers between devices with their start and end apart: 7 -> 7, of which waited for: 5 -> 5; matrix products, arithmetic and copies ran while one was open for 14% -> 15% of each run, Pallas kernels for 0% -> 0%
where the time goes in v1:
time: 480 us; the launch traced here: 473 us
  waiting for transfers between devices  118 us (25%)
  local copies, waits for them, and re-layouts  91.2 us (19%)
  matrix products  89.5 us (19%)
  starting transfers between devices  62.2 us (13%)
  other arithmetic  59.2 us (12%)
  blocking collectives  52.2 us (11%)
    all_to_all x1, waiting for transfers between devices, body(): lax.all_to_all(fields, 'az', split_axis=2, concat_axis=3, tiled=True)  75 us
    all_to_all x1, blocking collectives, body(): lax.all_to_all(jnp.stack(jnp.split(row_fields, lax.axis_size('az'), axis=...  52.2 us
    all_to_all x1, starting transfers between devices, body(): lax.all_to_all(spectra, ('az', 'col'), split_axis=0, concat_axis=1, tiled...  40.7 us
    dot_general x1, matrix products, body(): jnp.einsum('frtp,pqk->ktqfr', lax.all_to_all(fields, 'az', split_axis=2,...  33.1 us
    all_to_all x1, waiting for transfers between devices, body(): lax.all_to_all(spectra, ('az', 'col'), split_axis=0, concat_axis=1, tiled...  29.5 us
    unnamed x26, local copies, waits for them, and re-layouts  26.2 us
    all_to_all x2, local copies, waits for them, and re-layouts, body(): lax.all_to_all(fields, 'az', split_axis=2, concat_axis=3, tiled=True)  22.5 us
    dot_general x1, matrix products, body(): jnp.einsum('ktqr,qkp->rtp', grid_modes, inverse_table, precision=highest_...  19.7 us
  transfers between devices with their start and end apart: 7, of which 5 were waited for; matrix products, arithmetic and copies ran while one was open for 15% of the time, Pallas kernels for 0%

profile of v1, /device:TPU:0, one launch (start us, length us, event | category | flops | bytes accessed | tf_op | source)
XLA Modules:
  0.0 472.6 jit_solution(7304477396417364079)
XLA Ops:
  0.0 4.2 fusion.82
  4.2 2.3 copy.80
  6.5 1.7 collective-permute-start
  8.2 0.7 copy.81
  8.9 0.0 copy-start
  8.9 2.9 collective-permute-start.1
  11.7 4.7 %fusion.81 = (bf16[1,64,64,256]{3,2,1,0:T(8,128)(2,1)}, bf16[1,64,64,256]{3,2,1,0:T(8,128)(2,1)}) fusion(bf16[2,64,64,256]{3,2,1,0:T(8,128)(2,1)} %param.6), kind=kLoop, calls=%fused_computation.121 | loop fusion | bytes 8388608 | tf_op jit(solution)/shard_map/slice | solution.py:84
  16.5 0.0 copy-done
  16.5 4.4 copy.50
  20.9 0.0 collective-permute-done
  20.9 1.9 copy.46
  22.9 0.0 collective-permute-done.1
  22.9 2.9 copy.48
  25.8 0.0 copy-start.2
  25.8 1.2 pad_maximum_fusion.3
  27.0 0.1 collective-permute-start.2
  27.1 5.6 %collective-permute-start.3 = (f32[64,1,258]{2,0,1:T(8,128)S(1)}, f32[64,1,258]{2,0,1:T(8,128)S(1)}, u32[]{:S(2)}, u32[]{:S(2)}) collective-permute-start(f32[64,1,258]{2,0,1:T(8,128)S(1)} %get-tuple-element.6), channel_id=1, source_target_pairs={{1,0},{2,1},{3,2},{4,3},{5,4},{6,5},{7,6},{8,7},{9,8},{10,9},{11,1... | collective-permute-start | bytes 198152 | tf_op jit(solution)/shard_map/ppermute | solution.py:21
  32.7 2.1 collective-permute-done.2
  34.7 0.1 collective-permute-done.3
  34.9 0.0 copy-done.2
  34.9 0.0 copy-done.3
  34.9 3.1 maximum_multiply_fusion.1
  38.0 0.0 copy-done.1
  38.0 10.6 %fusion.20 = (f32[1,64,64,256]{3,1,0,2:T(8,128)S(1)}, f32[1,64,64,256]{3,1,0,2:T(8,128)}) fusion(f32[64,66,258]{2,0,1:T(8,128)S(1)} %maximum_multiply_fusion.1, bf16[1,64,64,256]{3,2,1,0:T(8,128)(2,1)} %get-tuple-element.10, bf16[1,64,64,256]{3,2,1,0:T(8,128)(2,1)} %get-tuple-element.9, f32[64]{0:T(128)S(1)} %multiply_add_fusion.1, ...), kind=kLoop, calls=%fused_computation.32 | loop fusion | flops 15728640 | bytes 33554688 | tf_op jit(solution)/shard_map/stack | solution.py:90
  48.7 6.2 %pad_maximum_fusion = f32[2,64,64,256]{3,1,0,2:T(8,128)} fusion(f32[1,64,64,256]{3,1,0,2:T(8,128)} %get-tuple-element.8, f32[1,64,64,256]{3,1,0,2:T(8,128)S(1)} %get-tuple-element.7), kind=kLoop, calls=%fused_computation.9 | loop fusion | flops 2097152 | bytes 16777216 | tf_op jit(solution)/shard_map/stack | solution.py:90
  54.9 5.4 %all-to-all-start = ((f32[2,64,64,256]{3,1,0,2:T(8,128)}), f32[2,64,64,256]{3,1,0,2:T(8,128)}, u32[]{:S(2)}, u32[]{:S(2)}) async-start(f32[2,64,64,256]{3,1,0,2:T(8,128)} %pad_maximum_fusion), calls=%async_computation | async-start | bytes 16777216 | tf_op jit(solution)/shard_map/all_to_all | solution.py:94
  60.3 0.0 copy-done.5
  60.3 0.1 copy.42
  60.5 0.1 reshape.397
  60.6 18.0 %fusion.47 = (f32[2048,1,512]{2,0,1:T(8,128)}, f32[2048,1,512]{2,0,1:T(8,128)}) fusion(s32[512]{0:T(512)S(1)} %reshape.397), kind=kLoop, calls=%fused_computation.68 | loop fusion | flops 15728640 | bytes 8390656 | tf_op jit(solution)/shard_map/cos | solution.py:43
  78.6 75.0 %all-to-all-done = f32[2,64,64,256]{3,1,0,2:T(8,128)} async-done(((f32[2,64,64,256]{3,1,0,2:T(8,128)}), f32[2,64,64,256]{3,1,0,2:T(8,128)}, u32[]{:S(2)}, u32[]{:S(2)}) %all-to-all-start) | async-done | bytes 8388640 | tf_op jit(solution)/shard_map/all_to_all | solution.py:94
  153.5 13.2 %copy.99 = f32[2,64,8,8,256]{4,2,1,3,0:T(8,128)} copy(f32[2,64,8,8,256]{4,1,0,3,2:T(8,128)} %bitcast.6) | data formatting | bytes 16777216 | tf_op jit(solution)/shard_map/all_to_all | solution.py:94
  166.7 9.3 %reshape.411 = f32[2,64,8,2048,1]{3,1,2,0,4:T(8,128)} reshape(f32[2,64,8,8,256]{4,3,1,2,0:T(8,128)} %bitcast.130) | data formatting | bytes 16777216 | tf_op jit(solution)/shard_map/all_to_all | solution.py:94
  176.1 33.1 %fusion.34 = f32[512,8,2,2,64]{0,4,1,3,2:T(8,128)S(1)} fusion(f32[2,64,8,2048,1]{3,1,2,0,4:T(8,128)} %reshape.411, f32[2048,1,512]{2,0,1:T(8,128)} %get-tuple-element.20, f32[2048,1,512]{2,0,1:T(8,128)} %get-tuple-element.19), kind=kOutput, calls=%fused_computation.55 | convolution fusion | flops 25773998080 | bytes 20971520 | tf_op jit(solution)/shard_map/frtp,pqk->ktqfr/dot_general | solution.py:92
  209.1 2.5 copy.56
  211.6 5.4 %copy.57 = f32[512,8,256]{2,1,0:T(8,128)} copy(f32[512,8,256]{0,2,1:T(8,128)} %bitcast.131) | data formatting | bytes 8388608 | tf_op jit(solution)/shard_map/reshape | solution.py:98
  217.0 40.7 %all-to-all-start.1 = ((f32[512,8,256]{2,1,0:T(8,128)}), f32[512,8,256]{2,1,0:T(8,128)}, u32[]{:S(2)}, u32[]{:S(2)}) async-start(f32[512,8,256]{2,1,0:T(8,128)} %copy.57), calls=%async_computation.1 | async-start | bytes 8388608 | tf_op jit(solution)/shard_map/all_to_all | solution.py:99
  257.8 13.0 %copy.74 = bf16[512,64,64,1]{2,1,3,0:T(8,128)(2,1)} copy(bf16[512,64,64,1]{0,2,1,3:T(8,128)(2,1)} %bitcast.137) | data formatting | bytes 8388608 | tf_op args[4]
  270.8 9.9 %fusion.40 = f32[1,1024]{1,0:T(1,128)S(1)} fusion(f32[512,1]{0,1:T(1,128)S(1)} %bitcast.140, s32[512]{0:T(512)S(1)} %iota_add_fusion, s32[1024]{0:T(1024)S(1)} %multiply_add_fusion), kind=kOutput, calls=%fused_computation.59 | convolution fusion | flops 13631488 | bytes 12288 | tf_op jit(solution)/shard_map/dot_general | solution.py:37
  280.7 0.2 broadcast_divide_fusion
  280.9 29.5 %all-to-all-done.1 = f32[512,8,256]{2,1,0:T(8,128)} async-done(((f32[512,8,256]{2,1,0:T(8,128)}), f32[512,8,256]{2,1,0:T(8,128)}, u32[]{:S(2)}, u32[]{:S(2)}) %all-to-all-start.1) | async-done | bytes 4194336 | tf_op jit(solution)/shard_map/all_to_all | solution.py:99
  310.4 2.7 copy.59
  313.1 0.0 copy-start.4
  313.1 0.6 bitcast_multiply_fusion
  313.7 1.6 copy-done.4
  315.3 3.5 fusion.84
  318.8 1.2 fusion.83
  319.9 2.1 copy.83
  322.0 1.8 copy.84
  323.8 16.9 %fusion.51 = f32[4,512,2,64]{3,0,2,1:T(4,128)} fusion(bf16[512,64,64,1]{2,1,3,0:T(8,128)(2,1)} %copy.74, f32[4,512,2,1,64]{4,0,2,1,3:T(4,128)} %copy.84, f32[4,512,2,1,64]{4,0,2,1,3:T(4,128)S(1)} %copy.83, f32[512,64]{1,0:T(8,128)S(1)} %broadcast_divide_fusion), kind=kOutput, calls=%fused_computation.73 | convolution fusion | flops 201850880 | bytes 7471104 | tf_op jit(solution)/shard_map/lrs,klqs->klqr/dot_general | solution.py:114
  340.7 1.9 copy.64
  342.6 6.4 %convolution_bitcast_fusion = f32[4,1024,128]{1,2,0:T(8,128)S(1)} fusion(f32[4,512,128]{1,2,0:T(8,128)S(1)} %bitcast.138, bf16[4,1024,512]{2,1,0:T(8,128)(2,1)} %param.8), kind=kOutput, calls=%fused_computation.72 | convolution fusion | flops 3221225472 | bytes 7340032 | tf_op jit(solution)/shard_map/ktl,klx->ktx/dot_general | solution.py:120
  349.0 1.8 copy.65
  350.8 1.8 copy.66
  352.7 2.7 copy.67
  355.3 5.8 %all-to-all-start.2 = ((f32[4,1024,128]{2,0,1:T(4,128)}), f32[4,1024,128]{2,0,1:T(4,128)S(1)}, u32[]{:S(2)}, u32[]{:S(2)}) async-start(f32[4,1024,128]{2,0,1:T(4,128)} %copy.67), calls=%async_computation.2 | async-start | bytes 4194304 | tf_op jit(solution)/shard_map/all_to_all | solution.py:128
  361.2 19.1 %cosine_multiply_fusion = (f32[1,512,2048]{2,1,0:T(8,128)}, f32[1,512,2048]{2,1,0:T(8,128)}) fusion(s32[512]{0:T(512)S(1)} %reshape.397, f32[512]{0:T(512)S(1)} %get-tuple-element.17, f32[512]{0:T(512)S(1)} %get-tuple-element.18), kind=kLoop, calls=%fused_computation.44 | loop fusion | flops 16777216 | bytes 8394752 | tf_op jit(solution)/shard_map/mul | solution.py:51
  380.3 11.3 %all-to-all-done.2 = f32[4,1024,128]{2,0,1:T(4,128)S(1)} async-done(((f32[4,1024,128]{2,0,1:T(4,128)}), f32[4,1024,128]{2,0,1:T(4,128)S(1)}, u32[]{:S(2)}, u32[]{:S(2)}) %all-to-all-start.2) | async-done | bytes 2097184 | tf_op jit(solution)/shard_map/all_to_all | solution.py:128
  391.6 0.1 copy.100
  391.8 0.3 copy.69
  392.1 3.7 reshape.405
  395.7 19.7 %fusion.31 = f32[64,8,2048]{2,0,1:T(8,128)S(1)} fusion(f32[512,8,2,64]{3,2,1,0:T(2,128)} %reshape.405, f32[1,512,2048]{2,1,0:T(8,128)} %get-tuple-element.16, f32[1,512,2048]{2,1,0:T(8,128)} %get-tuple-element.15), kind=kOutput, calls=%fused_computation.52 | convolution fusion | flops 12886999040 | bytes 14680064 | tf_op jit(solution)/shard_map/ktqr,qkp->rtp/dot_general | solution.py:131
  415.8 52.2 %all_to_all.53 = f32[8,64,8,256]{3,1,2,0:T(8,128)S(1)} all-to-all(f32[8,64,8,256]{3,1,2,0:T(8,128)S(1)} %fusion.61), channel_id=1, replica_groups=mesh['az'=8,'col'=16] {'az'}, dimensions={0} | all-to-all | bytes 8388608 | tf_op jit(solution)/shard_map/all_to_all | solution.py:133
  468.0 4.4 copy.71
  (20 shorter events, 0.4 us)
Async XLA Ops:
  6.5 14.5 %collective-permute-start = (f32[64,64,1]{1,0,2:T(8,128)S(1)}, f32[64,64,1]{1,0,2:T(8,128)S(1)}, u32[]{:S(2)}, u32[]{:S(2)}) collective-permute-start(f32[64,64,1]{1,0,2:T(8,128)S(1)} %copy.80), channel_id=1, source_target_pairs={{0,16},{16,32},{32,48},{48,64},{64,80},{80,96},{96,112},{112,0},{1... | collective-permute-start | bytes 49160 | tf_op jit(solution)/shard_map/ppermute | solution.py:18
  8.9 7.6 %copy-start = (f32[64,64,256]{2,1,0:T(8,128)S(1)}, f32[64,64,256]{2,1,0:T(8,128)}, u32[]{:S(2)}) copy-start(f32[64,64,256]{2,1,0:T(8,128)} %param.5) | copy-start | bytes 12582916
  8.9 14.0 %collective-permute-start.1 = (f32[64,64,1]{1,0,2:T(8,128)S(1)}, f32[64,64,1]{1,0,2:T(8,128)S(1)}, u32[]{:S(2)}, u32[]{:S(2)}) collective-permute-start(f32[64,64,1]{1,0,2:T(8,128)S(1)} %copy.81), channel_id=1, source_target_pairs={{16,0},{32,16},{48,32},{64,48},{80,64},{96,80},{112,96},{0,112},{1... | collective-permute-start | bytes 49160 | tf_op jit(solution)/shard_map/ppermute | solution.py:21
  25.8 9.1 %copy-start.2 = (f32[64,64,256]{2,0,1:T(8,128)S(1)}, f32[64,64,256]{2,0,1:T(8,128)}, u32[]{:S(2)}) copy-start(f32[64,64,256]{2,0,1:T(8,128)} %copy.50) | copy-start | bytes 12582916
  25.8 9.1 %copy-start.3 = (f32[64,64,1]{2,0,1:T(8,128)S(1)}, f32[64,64,1]{2,0,1:T(8,128)}, u32[]{:S(2)}) copy-start(f32[64,64,1]{2,0,1:T(8,128)} %copy.48) | copy-start | bytes 49156
  27.0 7.7 %collective-permute-start.2 = (f32[64,1,258]{2,0,1:T(8,128)S(1)}, f32[64,1,258]{2,0,1:T(8,128)S(1)}, u32[]{:S(2)}, u32[]{:S(2)}) collective-permute-start(f32[64,1,258]{2,0,1:T(8,128)S(1)} %get-tuple-element.5), channel_id=1, source_target_pairs={{0,1},{1,2},{2,3},{3,4},{4,5},{5,6},{6,7},{7,8},{8,9},{9,10},{10,1... | collective-permute-start | bytes 198152 | tf_op jit(solution)/shard_map/ppermute | solution.py:18
  27.1 7.8 %collective-permute-start.3 = (f32[64,1,258]{2,0,1:T(8,128)S(1)}, f32[64,1,258]{2,0,1:T(8,128)S(1)}, u32[]{:S(2)}, u32[]{:S(2)}) collective-permute-start(f32[64,1,258]{2,0,1:T(8,128)S(1)} %get-tuple-element.6), channel_id=1, source_target_pairs={{1,0},{2,1},{3,2},{4,3},{5,4},{6,5},{7,6},{8,7},{9,8},{10,9},{11,1... | collective-permute-start | bytes 198152 | tf_op jit(solution)/shard_map/ppermute | solution.py:21
  32.7 5.4 %copy-start.1 = (f32[64,64,256]{2,1,0:T(8,128)S(1)}, f32[64,64,256]{2,1,0:T(8,128)}, u32[]{:S(2)}) copy-start(f32[64,64,256]{2,1,0:T(8,128)} %param.5) | copy-start | bytes 12582916
  54.9 5.4 %copy-start.5 = (s32[128,4]{0,1:T(4,128)S(1)}, s32[128,4]{0,1:T(4,128)}, u32[]{:S(2)}) copy-start(s32[128,4]{0,1:T(4,128)} %param.7) | copy-start | bytes 6148
  54.9 98.6 %all-to-all-start = ((f32[2,64,64,256]{3,1,0,2:T(8,128)}), f32[2,64,64,256]{3,1,0,2:T(8,128)}, u32[]{:S(2)}, u32[]{:S(2)}) async-start(f32[2,64,64,256]{3,1,0,2:T(8,128)} %pad_maximum_fusion), calls=%async_computation | async-start | bytes 16777216 | tf_op jit(solution)/shard_map/all_to_all | solution.py:94
  217.0 93.4 %all-to-all-start.1 = ((f32[512,8,256]{2,1,0:T(8,128)}), f32[512,8,256]{2,1,0:T(8,128)}, u32[]{:S(2)}, u32[]{:S(2)}) async-start(f32[512,8,256]{2,1,0:T(8,128)} %copy.57), calls=%async_computation.1 | async-start | bytes 8388608 | tf_op jit(solution)/shard_map/all_to_all | solution.py:99
  313.1 2.2 copy-start.4
  355.3 36.3 %all-to-all-start.2 = ((f32[4,1024,128]{2,0,1:T(4,128)}), f32[4,1024,128]{2,0,1:T(4,128)S(1)}, u32[]{:S(2)}, u32[]{:S(2)}) async-start(f32[4,1024,128]{2,0,1:T(4,128)} %copy.67), calls=%async_computation.2 | async-start | bytes 4194304 | tf_op jit(solution)/shard_map/all_to_all | solution.py:128
